TPU v7x, 256 devices: a whole 4x4x8 slice. The times are simulated.
256 devices in a mesh: dp: 32 (over y, x, core), mp: 8 (over z).
Axes of the slice: x: 4, y: 4, z: 8, core: 2. Of those that a mesh axis runs over, the one named last changes fastest.
Arguments:
- activations: bfloat16 [4096, 2560], P('dp'), may hold values from -6 to 6
- grad_hidden: bfloat16 [4096, 8192], P('dp', 'mp'), may hold values from -0.059814453 to 0.059814453
- up_weight: bfloat16 [2560, 8192], P('dp', 'mp'), may hold values from -6 to 6
- error_feedback: bfloat16 [32, 2560, 8192], P('dp', None, 'mp'), may hold values from -0.75 to 0.75
- query_previous: float32 [8192, 128], P('mp'), may hold values from -6 to 6
Outputs:
- grad_input: bfloat16 [4096, 2560], P('dp', 'mp')
- error_next: bfloat16 [32, 2560, 8192], P('dp', None, 'mp')
- update: float32 [2560, 8192], P('dp', 'mp')
- query_next: float32 [8192, 128], P('mp')
All inputs are finite; a program needn't handle non-finite values.
Results may differ from a plain program's by a relative error of at most 0.0005.
Values may be sent and summed in bfloat16 or wider, within the bound.
No kernel may reach another device: no remote copies, remote signals or barrier semaphores. Data moves between devices by JAX's collectives and lax.ppermute only.
A program may use at most 128 MiB of HBM per device.

v0:
```python
import jax
import jax.numpy as jnp
from jax import lax
from jax.sharding import PartitionSpec as P

HIGHEST = lax.Precision.HIGHEST


def orthonormal(project, gram_matrix):
    factor = jnp.linalg.cholesky(gram_matrix)
    return lax.linalg.triangular_solve(
        factor, project, left_side=False, lower=True, transpose_a=True
    )


def local(activations, grad_hidden, up_weight, error_feedback, query_previous):
    replicas = lax.axis_size("dp")
    partial_input = lax.dot_general(
        grad_hidden,
        lax.all_gather(up_weight, "dp", axis=0, tiled=True),
        (((1,), (1,)), ((), ())),
        preferred_element_type=jnp.float32,
    )
    grad_input = lax.psum_scatter(partial_input, "mp", scatter_dimension=1, tiled=True).astype(
        jnp.bfloat16
    )
    local_grad = lax.dot_general(
        activations, grad_hidden, (((0,), (0,)), ((), ())), preferred_element_type=jnp.float32
    )
    merged = error_feedback[0].astype(jnp.float32) + local_grad
    project = jnp.dot(merged, query_previous, precision=HIGHEST, preferred_element_type=jnp.float32)
    project = lax.psum(project, ("dp", "mp"))
    gram_matrix = jnp.dot(project.T, project, precision=HIGHEST, preferred_element_type=jnp.float32)
    basis_full = orthonormal(project, gram_matrix)
    query_term = lax.dot_general(
        merged,
        basis_full,
        (((0,), (0,)), ((), ())),
        precision=HIGHEST,
        preferred_element_type=jnp.float32,
    )
    query_next = lax.psum(query_term, "dp") / replicas
    low_rank = lax.dot_general(
        basis_full,
        query_next,
        (((1,), (1,)), ((), ())),
        precision=HIGHEST,
        preferred_element_type=jnp.float32,
    )
    error_next = (merged - low_rank).astype(jnp.bfloat16)[None]
    row_share = merged.shape[0] // replicas
    update = lax.dynamic_slice_in_dim(low_rank, lax.axis_index("dp") * row_share, row_share, 0)
    return (grad_input, error_next, update, query_next)


def solution(mesh):
    in_specs = (P("dp", None), P("dp", "mp"), P("dp", "mp"), P("dp", None, "mp"), P("mp", None))
    out_specs = (P("dp", "mp"), P("dp", None, "mp"), P("dp", "mp"), P("mp", None))
    return jax.shard_map(local, mesh=mesh, in_specs=in_specs, out_specs=out_specs, check_vma=False)
```

profile of v0, /device:TPU:4, one launch (start us, length us, event | category | flops | bytes accessed | tf_op | source)
XLA Modules:
  0.0 501.2 jit_solution(10728935111397148013)
XLA Ops:
  8.0 0.0 copy-start
  8.0 0.0 all-reduce.3.cloned.1.call-start
  8.1 1.0 copy-done
  9.1 0.0 copy-start.5
  9.1 4.2 convert_add_fusion
  13.3 0.0 copy-start.1
  13.3 4.0 copy-done.1
  17.2 0.0 copy-done.5
  17.2 9.4 %fusion.6 = f32[2560,128]{1,0:T(8,128)} fusion(f32[2560,1024]{1,0:T(8,128)S(1)} %convert_add_fusion, f32[1024,128]{1,0:T(8,128)S(1)} %copy-done.5), kind=kOutput, calls=%fused_computation.16 | convolution fusion | flops 4026531840 | bytes 12320768 | tf_op jit(solution)/shard_map/dot_general | solution.py:31
  26.7 0.0 all-reduce.3.cloned.1.call-update
  26.7 0.0 all-gather.2.cloned.1.call-start
  26.7 0.5 all-gather.2.cloned.1.call-update
  27.3 0.5 all-reduce.5.cloned.1.call-start
  27.8 261.2 %all-reduce.3.cloned.1.call-done = f32[2560,128]{1,0:T(8,128)} async-done(((f32[2560,128]{1,0:T(8,128)}), f32[2560,128]{1,0:T(8,128)}) %all-reduce.3.cloned.1.call-update) | async-done | bytes 1310736 | tf_op jit(solution)/shard_map/psum | solution.py:32
  288.9 3.9 fusion.7
  292.9 0.1 copy.9
  293.0 11.7 %cholesky.16 = f32[128,128]{1,0:T(8,128)S(1)} custom-call(f32[128,128]{1,0:T(8,128)S(1)} %fusion.4), custom_call_target="Cholesky" | custom-call | tf_op jit(solution)/shard_map/jit(cholesky)/cholesky | solution.py:10
  304.7 0.6 compare_reduce_fusion
  305.4 0.7 fusion.1
  306.0 9.8 %custom-call.6 = f32[1,128,128]{1,2,0:T(8,128)S(1)} custom-call(f32[1,128,128]{2,1,0:T(8,128)S(1)} %fusion.1), custom_call_target="InvertDiagBlocksLowerTriangular" | custom-call | tf_op jit(solution)/shard_map/triangular_solve | solution.py:11
  315.9 2.5 fusion.2
  318.4 0.0 copy-start.4
  318.4 19.9 %fusion.8 = f32[1024,128]{1,0:T(8,128)} fusion(f32[2560,1024]{1,0:T(8,128)} %copy-done.1, f32[2560,128]{1,0:T(8,128)S(1)} %fusion.2), kind=kOutput, calls=%fused_computation.18 | convolution fusion | flops 4026531840 | bytes 12320768 | tf_op jit(solution)/shard_map/dot_general | solution.py:35
  338.3 0.0 all-reduce.5.cloned.1.call-update
  338.3 0.3 reduce-scatter.2.cloned.1.call-start
  338.6 0.0 all-gather.2.cloned.1.call-done
  338.6 0.0 copy-done.4
  338.6 5.1 %fusion.5 = f32[128,2560]{0,1:T(8,128)} fusion(bf16[128,1024]{1,0:T(8,128)(2,1)S(1)} %copy-done.4, bf16[2560,1024]{1,0:T(8,128)(2,1)} %all-gather.2.cloned.1.call-done), kind=kOutput, calls=%fused_computation.15 | convolution fusion | flops 671088640 | bytes 6815744 | tf_op jit(solution)/shard_map/dot_general | solution.py:18
  343.7 0.0 reduce-scatter.2.cloned.1.call-update
  343.7 106.1 %all-reduce.5.cloned.1.call-done = f32[1024,128]{1,0:T(8,128)} async-done(((f32[1024,128]{1,0:T(8,128)}), f32[1024,128]{1,0:T(8,128)}) %all-reduce.5.cloned.1.call-update) | async-done | bytes 524304 | tf_op jit(solution)/shard_map/psum | solution.py:42
  449.8 1.1 broadcast_multiply_fusion
  450.9 0.0 copy-start.3
  450.9 8.4 %fusion.9 = f32[2560,1024]{1,0:T(8,128)S(1)} fusion(f32[2560,128]{1,0:T(8,128)S(1)} %fusion.2, f32[1024,128]{1,0:T(8,128)S(1)} %broadcast_multiply_fusion), kind=kOutput, calls=%fused_computation.19 | convolution fusion | flops 4026531840 | bytes 12320768 | tf_op jit(solution)/shard_map/dot_general | solution.py:43
  459.4 0.0 copy-done.3
  459.4 0.0 copy-start.2
  459.4 3.8 copy-done.2
  463.2 0.7 constant_dynamic-slice_fusion
  464.0 11.5 %fusion = bf16[1,2560,1024]{2,1,0:T(8,128)(2,1)} fusion(f32[2560,1024]{1,0:T(8,128)} %copy-done.1, f32[2560,1024]{1,0:T(8,128)} %copy-done.2), kind=kLoop, calls=%fused_computation.2 | loop fusion | flops 5242880 | bytes 26214400 | tf_op jit(solution)/shard_map/broadcast_in_dim | solution.py:50
  475.5 16.3 %reduce-scatter.2.cloned.1.call-done = f32[128,320]{0,1:T(8,128)} async-done(((f32[128,2560]{0,1:T(8,128)}), f32[128,320]{0,1:T(8,128)}) %reduce-scatter.2.cloned.1.call-update) | async-done | bytes 163856 | tf_op jit(solution)/shard_map/reduce_scatter | solution.py:24
  491.8 1.6 convert_element_type.12
  (2 shorter events, 0.0 us)
Async XLA Ops:
  8.0 1.1 copy-start
  8.0 280.9 %all-reduce.3.cloned.1.call-start = ((), (), s32[]{:S(2)}) async-start(), calls=%async_computation.3 | async-start | bytes 2621440 | tf_op jit(solution)/shard_map/psum | solution.py:32
  9.1 8.2 %copy-start.5 = (f32[1024,128]{1,0:T(8,128)S(1)}, f32[1024,128]{1,0:T(8,128)}, u32[]{:S(2)}) copy-start(f32[1024,128]{1,0:T(8,128)} %param.9) | copy-start | bytes 1572868
  13.3 4.0 copy-start.1
  26.7 311.9 %all-gather.2.cloned.1.call-start = ((), (), s32[]{:S(2)}) async-start(), calls=%async_computation.1 | async-start | bytes 5406720 | tf_op jit(solution)/shard_map/all_gather | solution.py:20
  27.3 422.5 %all-reduce.5.cloned.1.call-start = ((), (), s32[]{:S(2)}) async-start(), calls=%async_computation.4 | async-start | bytes 1048576 | tf_op jit(solution)/shard_map/psum | solution.py:42
  318.4 20.3 %copy-start.4 = (bf16[128,1024]{1,0:T(8,128)(2,1)S(1)}, bf16[128,1024]{1,0:T(8,128)(2,1)}, u32[]{:S(2)}) copy-start(bf16[128,1024]{1,0:T(8,128)(2,1)} %param.6) | copy-start | bytes 786436
  338.3 153.5 %reduce-scatter.2.cloned.1.call-start = ((), (), s32[]{:S(2)}) async-start(), calls=%async_computation.2 | async-start | bytes 1474560 | tf_op jit(solution)/shard_map/reduce_scatter | solution.py:24
  450.9 8.5 %copy-start.3 = (f32[1024,128]{1,0:T(8,128)}, f32[1024,128]{1,0:T(8,128)S(1)}, u32[]{:S(2)}) copy-start(f32[1024,128]{1,0:T(8,128)S(1)} %broadcast_multiply_fusion) | copy-start | bytes 1572868
  459.4 3.8 copy-start.2
Sparse Core Ops, SparseCore 0:
  26.8 262.0 all-reduce.2
Sparse Core Ops, SparseCore 1:
  29.7 54.2 all-gather.1
  338.4 111.3 all-reduce.4
  452.2 39.5 reduce-scatter.1
where the time goes:
time: 509 us; the launch traced here: 501 us
  waiting for transfers between devices  384 us (75%)
  matrix products  53.5 us (11%)
  other arithmetic  37 us (7%)
  between operations  16 us (3%)
  local copies, waits for them, and re-layouts  9.68 us (2%)
    psum x1, waiting for transfers between devices, local(): project = lax.psum(project, ('dp', 'mp'))  261 us
    psum x1, waiting for transfers between devices, local(): query_next = lax.psum(query_term, 'dp') / replicas  106 us
    dot_general x1, matrix products, local(): lax.dot_general(merged, basis_full, (((0,), (0,)), ((), ())), precision=H...  19.9 us
    reduce_scatter x1, waiting for transfers between devices, local(): lax.psum_scatter(partial_input, 'mp', scatter_dimension=1, tiled=True)  16.3 us
    another operation x3, other arithmetic, orthonormal(): factor = jnp.linalg.cholesky(gram_matrix)  12.4 us
    broadcast_in_dim x1, other arithmetic, local(): error_next = (merged - low_rank).astype(jnp.bfloat16)[None]  11.5 us
    another operation x2, other arithmetic, orthonormal(): lax.linalg.triangular_solve(factor, project, left_side=False, lower=True,...  10.5 us
  transfers between devices with their start and end apart: 4, of which 3 were waited for; matrix products, arithmetic and copies ran while one was open for 15% of the time, Pallas kernels for 0%

commit v1 on v0

--- a/solution.py
+++ b/solution.py
@@ -39,7 +39,7 @@
         precision=HIGHEST,
         preferred_element_type=jnp.float32,
     )
-    query_next = lax.psum(query_term, "dp") / replicas
+    query_next = jnp.sum(lax.all_gather(query_term, "dp"), axis=0) / replicas
     low_rank = lax.dot_general(
         basis_full,
         query_next,

time: 509 us -> 463 us (0.910)
  waiting for transfers between devices: 384 us -> 333 us
  other arithmetic: 37 us -> 42.6 us
    psum x1 -> x0, waiting for transfers between devices: 106 us -> none  [local(): query_next = lax.psum(query_term, 'dp') / replicas]
    all_gather x0 -> x1, waiting for transfers between devices: none -> 74.8 us  [local(): query_next = jnp.sum(lax.all_gather(query_term, 'dp'), axis=0) / replicas]
    psum x1, waiting for transfers between devices: 261 us -> 219 us  [local(): project = lax.psum(project, ('dp', 'mp'))]
    all_gather x1, waiting for transfers between devices: 0.02 us -> 38.6 us  [local(): lax.all_gather(up_weight, 'dp', axis=0, tiled=True)]
    reduce_scatter x1, waiting for transfers between devices: 16.3 us -> 0.02 us  [local(): lax.psum_scatter(partial_input, 'mp', scatter_dimension=1, tiled=True)]
    reduce_sum x0 -> x1, other arithmetic: none -> 6.57 us  [local(): query_next = jnp.sum(lax.all_gather(query_term, 'dp'), axis=0) / replicas]
where the time goes in v1:
time: 463 us; the launch traced here: 454 us
  waiting for transfers between devices  333 us (72%)
  matrix products  56.1 us (12%)
  other arithmetic  42.6 us (9%)
  between operations  15.5 us (3%)
  local copies, waits for them, and re-layouts  6.08 us (1%)
    psum x1, waiting for transfers between devices, local(): project = lax.psum(project, ('dp', 'mp'))  219 us
    all_gather x1, waiting for transfers between devices, local(): query_next = jnp.sum(lax.all_gather(query_term, 'dp'), axis=0) / replicas  74.8 us
    all_gather x1, waiting for transfers between devices, local(): lax.all_gather(up_weight, 'dp', axis=0, tiled=True)  38.6 us
    dot_general x1, matrix products, local(): lax.dot_general(merged, basis_full, (((0,), (0,)), ((), ())), precision=H...  19.9 us
    another operation x3, other arithmetic, orthonormal(): factor = jnp.linalg.cholesky(gram_matrix)  12.4 us
    broadcast_in_dim x1, other arithmetic, local(): error_next = (merged - low_rank).astype(jnp.bfloat16)[None]  11.6 us
    dot_general x1, matrix products, local(): lax.dot_general(basis_full, query_next, (((1,), (1,)), ((), ())), precisi...  11 us
    another operation x2, other arithmetic, orthonormal(): lax.linalg.triangular_solve(factor, project, left_side=False, lower=True,...  10.5 us
  transfers between devices with their start and end apart: 4, of which 3 were waited for; matrix products, arithmetic and copies ran while one was open for 15% of the time, Pallas kernels for 0%

profile of v1, /device:TPU:4, one launch (start us, length us, event | category | flops | bytes accessed | tf_op | source)
XLA Modules:
  0.0 453.8 jit_solution(15477925856506508915)
XLA Ops:
  8.0 0.0 copy-start
  8.0 0.0 all-gather.4.cloned.1.call-start
  8.1 0.7 all-gather.4.cloned.1.call-update
  8.7 0.0 copy-start.4
  8.8 0.0 all-reduce.2.cloned.1.call-start
  8.8 0.3 copy-done
  9.1 4.1 convert_add_fusion
  13.2 0.0 copy-start.1
  13.2 4.0 copy-done.1
  17.2 0.0 copy-done.4
  17.2 0.0 copy-start.3
  17.2 9.4 %fusion.6 = f32[2560,128]{1,0:T(8,128)} fusion(f32[2560,1024]{1,0:T(8,128)S(1)} %convert_add_fusion, f32[1024,128]{1,0:T(8,128)S(1)} %copy-done.4), kind=kOutput, calls=%fused_computation.16 | convolution fusion | flops 4026531840 | bytes 12320768 | tf_op jit(solution)/shard_map/dot_general | solution.py:31
  26.6 0.0 all-reduce.2.cloned.1.call-update
  26.7 0.5 reduce-scatter.2.cloned.1.call-start
  27.2 38.6 %all-gather.4.cloned.1.call-done = bf16[2560,1024]{1,0:T(8,128)(2,1)} async-done(((bf16[80,1024]{1,0:T(8,128)(2,1)}), bf16[2560,1024]{1,0:T(8,128)(2,1)}) %all-gather.4.cloned.1.call-update) | async-done | bytes 5242896 | tf_op jit(solution)/shard_map/all_gather | solution.py:20
  65.7 0.0 copy-done.3
  65.7 5.1 %fusion.5 = f32[128,2560]{0,1:T(8,128)} fusion(bf16[128,1024]{1,0:T(8,128)(2,1)S(1)} %copy-done.3, bf16[2560,1024]{1,0:T(8,128)(2,1)} %all-gather.4.cloned.1.call-done), kind=kOutput, calls=%fused_computation.15 | convolution fusion | flops 671088640 | bytes 6815744 | tf_op jit(solution)/shard_map/dot_general | solution.py:18
  70.8 0.0 reduce-scatter.2.cloned.1.call-update
  70.9 0.0 all-gather.6.cloned.1.call-start
  70.9 218.7 %all-reduce.2.cloned.1.call-done = f32[2560,128]{1,0:T(8,128)} async-done(((f32[2560,128]{1,0:T(8,128)}), f32[2560,128]{1,0:T(8,128)}) %all-reduce.2.cloned.1.call-update) | async-done | bytes 1310736 | tf_op jit(solution)/shard_map/psum | solution.py:32
  289.6 4.0 fusion.7
  293.6 0.1 copy.9
  293.8 11.7 %cholesky.16 = f32[128,128]{1,0:T(8,128)S(1)} custom-call(f32[128,128]{1,0:T(8,128)S(1)} %fusion.4), custom_call_target="Cholesky" | custom-call | tf_op jit(solution)/shard_map/jit(cholesky)/cholesky | solution.py:10
  305.5 0.6 compare_reduce_fusion
  306.1 0.7 fusion.1
  306.8 9.8 %custom-call.6 = f32[1,128,128]{1,2,0:T(8,128)S(1)} custom-call(f32[1,128,128]{2,1,0:T(8,128)S(1)} %fusion.1), custom_call_target="InvertDiagBlocksLowerTriangular" | custom-call | tf_op jit(solution)/shard_map/triangular_solve | solution.py:11
  316.6 2.5 fusion.2
  319.1 19.9 %fusion.8 = f32[1024,128]{1,0:T(8,128)} fusion(f32[2560,1024]{1,0:T(8,128)} %copy-done.1, f32[2560,128]{1,0:T(8,128)S(1)} %fusion.2), kind=kOutput, calls=%fused_computation.18 | convolution fusion | flops 4026531840 | bytes 12320768 | tf_op jit(solution)/shard_map/dot_general | solution.py:35
  339.1 0.0 all-gather.6.cloned.1.call-update
  339.1 0.0 reduce-scatter.2.cloned.1.call-done
  339.1 1.6 convert_element_type.12
  340.7 74.8 %all-gather.6.cloned.1.call-done = f32[32768,128]{1,0:T(8,128)} async-done(((f32[1024,128]{1,0:T(8,128)}), f32[32768,128]{1,0:T(8,128)}) %all-gather.6.cloned.1.call-update) | async-done | bytes 16777232 | tf_op jit(solution)/shard_map/all_gather | solution.py:42
  415.5 6.6 %reduce_sum.9 = f32[1024,128]{1,0:T(8,128)S(1)} reduce(f32[32,1024,128]{2,1,0:T(8,128)} %bitcast.28, f32[]{:T(128)} %constant.48.clone.1), dimensions={0}, to_apply=%region_4.5 | reduce | flops 4063232 | bytes 17301508 | tf_op jit(solution)/shard_map/reduce_sum | solution.py:42
  422.1 0.0 copy-start.2
  422.1 11.0 %fusion.9 = f32[2560,1024]{1,0:T(8,128)} fusion(f32[2560,128]{1,0:T(8,128)S(1)} %fusion.2, f32[1024,128]{1,0:T(8,128)S(1)} %broadcast_multiply_fusion), kind=kOutput, calls=%fused_computation.19 | convolution fusion | flops 4026531840 | bytes 12320768 | tf_op jit(solution)/shard_map/dot_general | solution.py:43
  433.1 0.0 copy-done.2
  433.1 11.6 %fusion = bf16[1,2560,1024]{2,1,0:T(8,128)(2,1)} fusion(f32[2560,1024]{1,0:T(8,128)} %copy-done.1, f32[2560,1024]{1,0:T(8,128)} %fusion.9), kind=kLoop, calls=%fused_computation.2 | loop fusion | flops 5242880 | bytes 26214400 | tf_op jit(solution)/shard_map/broadcast_in_dim | solution.py:50
  444.7 1.7 constant_dynamic-slice_fusion
  (3 shorter events, 0.1 us)
Async XLA Ops:
  8.0 1.1 copy-start
  8.0 57.7 %all-gather.4.cloned.1.call-start = ((), (), s32[]{:S(2)}) async-start(), calls=%async_computation.1 | async-start | bytes 5406720 | tf_op jit(solution)/shard_map/all_gather | solution.py:20
  8.7 8.5 %copy-start.4 = (f32[1024,128]{1,0:T(8,128)S(1)}, f32[1024,128]{1,0:T(8,128)}, u32[]{:S(2)}) copy-start(f32[1024,128]{1,0:T(8,128)} %param.9) | copy-start | bytes 1572868
  8.8 280.8 %all-reduce.2.cloned.1.call-start = ((), (), s32[]{:S(2)}) async-start(), calls=%async_computation.3 | async-start | bytes 2621440 | tf_op jit(solution)/shard_map/psum | solution.py:32
  13.2 4.0 copy-start.1
  17.2 48.5 %copy-start.3 = (bf16[128,1024]{1,0:T(8,128)(2,1)S(1)}, bf16[128,1024]{1,0:T(8,128)(2,1)}, u32[]{:S(2)}) copy-start(bf16[128,1024]{1,0:T(8,128)(2,1)} %param.6) | copy-start | bytes 786436
  26.7 312.5 %reduce-scatter.2.cloned.1.call-start = ((), (), s32[]{:S(2)}) async-start(), calls=%async_computation.2 | async-start | bytes 1474560 | tf_op jit(solution)/shard_map/reduce_scatter | solution.py:24
  70.9 344.6 %all-gather.6.cloned.1.call-start = ((), (), s32[]{:S(2)}) async-start(), calls=%async_computation.4 | async-start | bytes 17301504 | tf_op jit(solution)/shard_map/all_gather | solution.py:42
  422.1 11.1 %copy-start.2 = (f32[1024,128]{1,0:T(8,128)}, f32[1024,128]{1,0:T(8,128)S(1)}, u32[]{:S(2)}) copy-start(f32[1024,128]{1,0:T(8,128)S(1)} %broadcast_multiply_fusion) | copy-start | bytes 1572868
Sparse Core Ops, SparseCore 0:
  11.4 54.3 all-gather.3
  71.0 40.3 reduce-scatter.1
  339.2 76.2 all-gather.5
Sparse Core Ops, SparseCore 1:
  26.7 262.8 all-reduce.1

commit v2 on v0

--- a/solution.py
+++ b/solution.py
@@ -29,7 +29,7 @@
     )
     merged = error_feedback[0].astype(jnp.float32) + local_grad
     project = jnp.dot(merged, query_previous, precision=HIGHEST, preferred_element_type=jnp.float32)
-    project = lax.psum(project, ("dp", "mp"))
+    project = lax.psum(lax.psum(project, "mp"), "dp")
     gram_matrix = jnp.dot(project.T, project, precision=HIGHEST, preferred_element_type=jnp.float32)
     basis_full = orthonormal(project, gram_matrix)
     query_term = lax.dot_general(

time: 509 us -> 452 us (0.89)
  waiting for transfers between devices: 384 us -> 329 us
    psum x1 -> x2, waiting for transfers between devices: 261 us -> 195 us  [local(): project = lax.psum(lax.psum(project, 'mp'), 'dp')]
    psum x1, waiting for transfers between devices: 106 us -> 112 us  [local(): query_next = lax.psum(query_term, 'dp') / replicas]
  transfers between devices with their start and end apart: 4 -> 5, of which waited for: 3 -> 5; matrix products, arithmetic and copies ran while one was open for 15% -> 17% of each run, Pallas kernels for 0% -> 0%
where the time goes in v2:
time: 452 us; the launch traced here: 445 us
  waiting for transfers between devices  329 us (73%)
  matrix products  53.5 us (12%)
  other arithmetic  37.1 us (8%)
  between operations  14.1 us (3%)
  local copies, waits for them, and re-layouts  9.68 us (2%)
    psum x2, waiting for transfers between devices, local(): project = lax.psum(lax.psum(project, 'mp'), 'dp')  195 us
    psum x1, waiting for transfers between devices, local(): query_next = lax.psum(query_term, 'dp') / replicas  112 us
    dot_general x1, matrix products, local(): lax.dot_general(merged, basis_full, (((0,), (0,)), ((), ())), precision=H...  19.9 us
    reduce_scatter x1, waiting for transfers between devices, local(): lax.psum_scatter(partial_input, 'mp', scatter_dimension=1, tiled=True)  16.4 us
    another operation x3, other arithmetic, orthonormal(): factor = jnp.linalg.cholesky(gram_matrix)  12.4 us
    broadcast_in_dim x1, other arithmetic, local(): error_next = (merged - low_rank).astype(jnp.bfloat16)[None]  11.6 us
    another operation x2, other arithmetic, orthonormal(): lax.linalg.triangular_solve(factor, project, left_side=False, lower=True,...  10.5 us
    dot_general x1, matrix products, local(): jnp.dot(merged, query_previous, precision=HIGHEST, preferred_element_type...  9.42 us
  transfers between devices with their start and end apart: 5, of which 5 were waited for; matrix products, arithmetic and copies ran while one was open for 17% of the time, Pallas kernels for 0%

profile of v2, /device:TPU:4, one launch (start us, length us, event | category | flops | bytes accessed | tf_op | source)
XLA Modules:
  0.0 444.7 jit_solution(10955744295953823353)
XLA Ops:
  7.2 0.0 copy-start
  7.2 0.0 all-reduce.4.cloned.1.call-start
  7.2 1.0 copy-done
  8.3 0.0 copy-start.5
  8.3 4.2 convert_add_fusion
  12.4 0.0 copy-start.1
  12.5 4.0 copy-done.1
  16.4 0.0 copy-done.5
  16.4 9.4 %fusion.6 = f32[2560,128]{1,0:T(8,128)} fusion(f32[2560,1024]{1,0:T(8,128)S(1)} %convert_add_fusion, f32[1024,128]{1,0:T(8,128)S(1)} %copy-done.5), kind=kOutput, calls=%fused_computation.16 | convolution fusion | flops 4026531840 | bytes 12320768 | tf_op jit(solution)/shard_map/dot_general | solution.py:31
  25.8 0.0 all-reduce.4.cloned.1.call-update
  25.9 0.0 all-reduce.6.cloned.1.call-start
  25.9 80.2 %all-reduce.4.cloned.1.call-done = f32[2560,128]{1,0:T(8,128)} async-done(((f32[2560,128]{1,0:T(8,128)}), f32[2560,128]{1,0:T(8,128)}) %all-reduce.4.cloned.1.call-update) | async-done | bytes 1310736 | tf_op jit(solution)/shard_map/psum | solution.py:32
  106.1 0.0 all-reduce.6.cloned.1.call-update
  106.2 0.0 all-gather.2.cloned.1.call-start
  106.2 0.7 all-gather.2.cloned.1.call-update
  106.9 0.5 all-reduce.8.cloned.1.call-start
  107.4 115.3 %all-reduce.6.cloned.1.call-done = f32[2560,128]{1,0:T(8,128)} async-done(((f32[2560,128]{1,0:T(8,128)}), f32[2560,128]{1,0:T(8,128)}) %all-reduce.6.cloned.1.call-update) | async-done | bytes 1310736 | tf_op jit(solution)/shard_map/psum | solution.py:32
  222.7 3.9 fusion.7
  226.6 0.1 copy.9
  226.7 11.7 %cholesky.16 = f32[128,128]{1,0:T(8,128)S(1)} custom-call(f32[128,128]{1,0:T(8,128)S(1)} %fusion.4), custom_call_target="Cholesky" | custom-call | tf_op jit(solution)/shard_map/jit(cholesky)/cholesky | solution.py:10
  238.5 0.6 compare_reduce_fusion
  239.1 0.7 fusion.1
  239.8 9.8 %custom-call.6 = f32[1,128,128]{1,2,0:T(8,128)S(1)} custom-call(f32[1,128,128]{2,1,0:T(8,128)S(1)} %fusion.1), custom_call_target="InvertDiagBlocksLowerTriangular" | custom-call | tf_op jit(solution)/shard_map/triangular_solve | solution.py:11
  249.6 2.5 fusion.2
  252.1 0.0 copy-start.4
  252.1 19.9 %fusion.8 = f32[1024,128]{1,0:T(8,128)} fusion(f32[2560,1024]{1,0:T(8,128)} %copy-done.1, f32[2560,128]{1,0:T(8,128)S(1)} %fusion.2), kind=kOutput, calls=%fused_computation.18 | convolution fusion | flops 4026531840 | bytes 12320768 | tf_op jit(solution)/shard_map/dot_general | solution.py:35
  272.0 0.0 all-reduce.8.cloned.1.call-update
  272.1 0.3 reduce-scatter.2.cloned.1.call-start
  272.3 4.8 %all-gather.2.cloned.1.call-done = bf16[2560,1024]{1,0:T(8,128)(2,1)} async-done(((bf16[80,1024]{1,0:T(8,128)(2,1)}), bf16[2560,1024]{1,0:T(8,128)(2,1)}) %all-gather.2.cloned.1.call-update) | async-done | bytes 5242896 | tf_op jit(solution)/shard_map/all_gather | solution.py:20
  277.1 0.0 copy-done.4
  277.1 5.1 %fusion.5 = f32[128,2560]{0,1:T(8,128)} fusion(bf16[128,1024]{1,0:T(8,128)(2,1)S(1)} %copy-done.4, bf16[2560,1024]{1,0:T(8,128)(2,1)} %all-gather.2.cloned.1.call-done), kind=kOutput, calls=%fused_computation.15 | convolution fusion | flops 671088640 | bytes 6815744 | tf_op jit(solution)/shard_map/dot_general | solution.py:18
  282.2 0.0 reduce-scatter.2.cloned.1.call-update
  282.2 112.1 %all-reduce.8.cloned.1.call-done = f32[1024,128]{1,0:T(8,128)} async-done(((f32[1024,128]{1,0:T(8,128)}), f32[1024,128]{1,0:T(8,128)}) %all-reduce.8.cloned.1.call-update) | async-done | bytes 524304 | tf_op jit(solution)/shard_map/psum | solution.py:42
  394.3 1.1 broadcast_multiply_fusion
  395.4 0.0 copy-start.3
  395.4 8.4 %fusion.9 = f32[2560,1024]{1,0:T(8,128)S(1)} fusion(f32[2560,128]{1,0:T(8,128)S(1)} %fusion.2, f32[1024,128]{1,0:T(8,128)S(1)} %broadcast_multiply_fusion), kind=kOutput, calls=%fused_computation.19 | convolution fusion | flops 4026531840 | bytes 12320768 | tf_op jit(solution)/shard_map/dot_general | solution.py:43
  403.9 0.0 copy-done.3
  403.9 0.0 copy-start.2
  403.9 3.8 copy-done.2
  407.7 0.7 constant_dynamic-slice_fusion
  408.5 11.6 %fusion = bf16[1,2560,1024]{2,1,0:T(8,128)(2,1)} fusion(f32[2560,1024]{1,0:T(8,128)} %copy-done.1, f32[2560,1024]{1,0:T(8,128)} %copy-done.2), kind=kLoop, calls=%fused_computation.2 | loop fusion | flops 5242880 | bytes 26214400 | tf_op jit(solution)/shard_map/broadcast_in_dim | solution.py:50
  420.0 16.4 %reduce-scatter.2.cloned.1.call-done = f32[128,320]{0,1:T(8,128)} async-done(((f32[128,2560]{0,1:T(8,128)}), f32[128,320]{0,1:T(8,128)}) %reduce-scatter.2.cloned.1.call-update) | async-done | bytes 163856 | tf_op jit(solution)/shard_map/reduce_scatter | solution.py:24
  436.4 1.6 convert_element_type.12
  (2 shorter events, 0.0 us)
Async XLA Ops:
  7.2 1.1 copy-start
  7.2 99.0 %all-reduce.4.cloned.1.call-start = ((), (), s32[]{:S(2)}) async-start(), calls=%async_computation.3 | async-start | bytes 2621440 | tf_op jit(solution)/shard_map/psum | solution.py:32
  8.3 8.2 %copy-start.5 = (f32[1024,128]{1,0:T(8,128)S(1)}, f32[1024,128]{1,0:T(8,128)}, u32[]{:S(2)}) copy-start(f32[1024,128]{1,0:T(8,128)} %param.9) | copy-start | bytes 1572868
  12.4 4.0 copy-start.1
  25.9 196.8 %all-reduce.6.cloned.1.call-start = ((), (), s32[]{:S(2)}) async-start(), calls=%async_computation.4 | async-start | bytes 2621440 | tf_op jit(solution)/shard_map/psum | solution.py:32
  106.2 170.9 %all-gather.2.cloned.1.call-start = ((), (), s32[]{:S(2)}) async-start(), calls=%async_computation.1 | async-start | bytes 5406720 | tf_op jit(solution)/shard_map/all_gather | solution.py:20
  106.9 287.4 %all-reduce.8.cloned.1.call-start = ((), (), s32[]{:S(2)}) async-start(), calls=%async_computation.5 | async-start | bytes 1048576 | tf_op jit(solution)/shard_map/psum | solution.py:42
  252.1 25.0 %copy-start.4 = (bf16[128,1024]{1,0:T(8,128)(2,1)S(1)}, bf16[128,1024]{1,0:T(8,128)(2,1)}, u32[]{:S(2)}) copy-start(bf16[128,1024]{1,0:T(8,128)(2,1)} %param.6) | copy-start | bytes 786436
  272.1 164.3 %reduce-scatter.2.cloned.1.call-start = ((), (), s32[]{:S(2)}) async-start(), calls=%async_computation.2 | async-start | bytes 1474560 | tf_op jit(solution)/shard_map/reduce_scatter | solution.py:24
  395.4 8.5 %copy-start.3 = (f32[1024,128]{1,0:T(8,128)}, f32[1024,128]{1,0:T(8,128)S(1)}, u32[]{:S(2)}) copy-start(f32[1024,128]{1,0:T(8,128)S(1)} %broadcast_multiply_fusion) | copy-start | bytes 1572868
  403.9 3.8 copy-start.2
Sparse Core Ops, SparseCore 0:
  26.0 80.1 all-reduce.3
  109.4 113.1 all-reduce.5
  225.2 51.8 all-gather.1
  280.7 113.5 all-reduce.7
  396.9 39.4 reduce-scatter.1
